TPU v7x, 32 devices: a whole 2x2x4 slice. The times are simulated.
32 devices in a mesh: groups: 2 (over y), seq: 8 (over z, x), head: 2 (over core).
Axes of the slice: x: 2, y: 2, z: 4, core: 2. Of those that a mesh axis runs over, the one named last changes fastest.
Arguments:
- queries: bfloat16 [2048, 1024], P(('groups', 'seq'), 'head'), parts along dimension 0, may hold values from -600 to 600
- keys: bfloat16 [2048, 1024], P(('groups', 'seq'), 'head'), parts along dimension 0, may hold values from -600 to 600
- values: bfloat16 [2048, 1024], P(('groups', 'seq'), 'head'), parts along dimension 0, may hold values from -600 to 600
- out_weight: bfloat16 [2048, 1024], P('seq', 'head'), may hold values from -0.1875 to 0.1875
- grad_y: bfloat16 [2048, 2048], P(('groups', 'seq')), parts along dimension 0, may hold values from -6 to 6
Outputs:
- out_y: bfloat16 [2048, 2048], P(('groups', 'seq')), parts along dimension 0
- grad_queries: bfloat16 [2048, 1024], P(('groups', 'seq'), 'head'), parts along dimension 0
- grad_keys: bfloat16 [2048, 1024], P(('groups', 'seq'), 'head'), parts along dimension 0
- grad_values: bfloat16 [2048, 1024], P(('groups', 'seq'), 'head'), parts along dimension 0
- grad_weight: float32 [4096, 1024], P(('groups', 'seq'), 'head'), parts along dimension 0
There are 2 independent parts, one for each index of `groups`. A program takes and returns all parts, laid end to end along the dimension named above; an argument that names none is the same for every part. Nothing has to cross between parts.
All inputs are finite; a program needn't handle non-finite values.
Results may differ from a plain program's by a relative error of at most 0.009.
Values may be sent and summed in bfloat16 or wider, within the bound.
No kernel may reach another device: no remote copies, remote signals or barrier semaphores. Data moves between devices by JAX's collectives and lax.ppermute only.
A program may use at most 192 MiB of HBM per device.

v0:
```python
import jax
import jax.numpy as jnp
from jax import lax
from jax.sharding import PartitionSpec as P

DH = 128
TILE = 128
epsilon = 1e-06


def carried_in(value, axis, join, neutral, backward):
    count, mine = (lax.axis_size(axis), lax.axis_index(axis))
    pieces = lax.all_gather(value, axis)
    if backward:
        pieces = pieces[::-1]
        mine = count - 1 - mine
    so_far = jnp.full_like(value, 0) + jnp.asarray(neutral, value.dtype)

    def turn(position, so_far):
        longer = join(so_far, pieces[position])
        return jnp.where(position < mine, longer, so_far)

    return lax.fori_loop(0, count - 1, turn, so_far)


def add_states(earlier, later):
    return earlier + later


def on_device(queries, keys, values, out_weight, grad_y):
    row_count = queries.shape[0]
    tile_count = row_count // TILE
    head_count = queries.shape[1] // DH

    def tiled(array):
        return array.reshape(tile_count, TILE, head_count, DH)

    query_tiles = tiled(queries)
    key_tiles = tiled(keys)
    value_tiles = tiled(values)
    causal = lax.broadcasted_iota(jnp.int32, (TILE, TILE), 0) >= lax.broadcasted_iota(
        jnp.int32, (TILE, TILE), 1
    )
    raw_scores = jnp.einsum(
        "nthd,nshd->nhts", query_tiles, key_tiles, preferred_element_type=jnp.float32
    )
    scores = jnp.where(causal, raw_scores, 0.0).astype(jnp.bfloat16)
    states = jnp.einsum(
        "nshd,nshe->nhde", key_tiles, value_tiles, preferred_element_type=jnp.float32
    )
    empty_state = jnp.zeros(states.shape[1:], jnp.float32)
    device_prefix = carried_in(jnp.sum(states, axis=0), "seq", add_states, empty_state, False)
    prefix_state = (device_prefix[None] + (jnp.cumsum(states, axis=0) - states)).astype(
        jnp.bfloat16
    )
    attended = jnp.einsum(
        "nhts,nshe->nthe", scores, value_tiles, preferred_element_type=jnp.float32
    )
    attended = attended + jnp.einsum(
        "nthd,nhde->nthe", query_tiles, prefix_state, preferred_element_type=jnp.float32
    )
    inverse_rms = lax.rsqrt(jnp.mean(attended * attended, axis=-1, keepdims=True) + epsilon)
    normed_exact = attended * inverse_rms
    normed = normed_exact.astype(jnp.bfloat16).reshape(row_count, -1)
    contract_last = (((1,), (1,)), ((), ()))
    back_weight = lax.all_gather(out_weight, "seq", axis=0, tiled=True)
    grad_normed = jnp.dot(grad_y, back_weight, preferred_element_type=jnp.float32)
    fore_weight = lax.all_gather(out_weight, "seq", axis=0, tiled=True)
    partial_out = lax.dot_general(
        normed, fore_weight, contract_last, preferred_element_type=jnp.float32
    )
    out_y = lax.psum(partial_out.astype(jnp.bfloat16), "head")
    grad_tiles = tiled(grad_normed)
    projected = jnp.mean(grad_tiles * normed_exact, axis=-1, keepdims=True)
    grad_out = (inverse_rms * (grad_tiles - normed_exact * projected)).astype(jnp.bfloat16)
    raw_grad = jnp.einsum(
        "nthe,nshe->nhts", grad_out, value_tiles, preferred_element_type=jnp.float32
    )
    grad_scores = jnp.where(causal, raw_grad, 0.0).astype(jnp.bfloat16)
    adjoint = jnp.einsum(
        "nthd,nthe->nhde", query_tiles, grad_out, preferred_element_type=jnp.float32
    )
    own_adjoint = jnp.sum(adjoint, axis=0)
    device_suffix = carried_in(own_adjoint, "seq", add_states, empty_state, True)
    later_tiles = jnp.flip(jnp.cumsum(jnp.flip(adjoint, 0), axis=0), 0) - adjoint
    suffix_state = (device_suffix[None] + later_tiles).astype(jnp.bfloat16)
    grad_queries = jnp.einsum(
        "nhts,nshd->nthd", grad_scores, key_tiles, preferred_element_type=jnp.float32
    )
    grad_queries = grad_queries + jnp.einsum(
        "nthe,nhde->nthd", grad_out, prefix_state, preferred_element_type=jnp.float32
    )
    grad_keys = jnp.einsum(
        "nhts,nthd->nshd", grad_scores, query_tiles, preferred_element_type=jnp.float32
    )
    grad_keys = grad_keys + jnp.einsum(
        "nshe,nhde->nshd", value_tiles, suffix_state, preferred_element_type=jnp.float32
    )
    grad_values = jnp.einsum(
        "nhts,nthe->nshe", scores, grad_out, preferred_element_type=jnp.float32
    )
    grad_values = grad_values + jnp.einsum(
        "nshd,nhde->nshe", key_tiles, suffix_state, preferred_element_type=jnp.float32
    )
    grad_weight = lax.psum_scatter(
        lax.dot_general(
            grad_y, normed, (((0,), (0,)), ((), ())), preferred_element_type=jnp.float32
        ),
        "seq",
        scatter_dimension=0,
        tiled=True,
    )
    return (
        out_y,
        grad_queries.reshape(row_count, -1).astype(jnp.bfloat16),
        grad_keys.reshape(row_count, -1).astype(jnp.bfloat16),
        grad_values.reshape(row_count, -1).astype(jnp.bfloat16),
        grad_weight,
    )


def solution(mesh):
    placed = (
        P(("groups", "seq"), "head"),
        P(("groups", "seq"), "head"),
        P(("groups", "seq"), "head"),
        P("seq", "head"),
        P(("groups", "seq"), None),
    )
    return jax.shard_map(
        on_device,
        mesh=mesh,
        in_specs=placed,
        out_specs=(
            P(("groups", "seq"), None),
            P(("groups", "seq"), "head"),
            P(("groups", "seq"), "head"),
            P(("groups", "seq"), "head"),
            P(("groups", "seq"), "head"),
        ),
        check_vma=False,
    )
```

profile of v0, /device:TPU:0, one launch (start us, length us, event | category | flops | bytes accessed | tf_op | source)
XLA Modules:
  0.0 284.6 jit_solution(14528810327368836696)
XLA Ops:
  7.2 1.1 copy.104
  8.3 1.8 fusion.10
  11.0 1.2 fusion.1
  12.8 1.1 convolution_bitcast_fusion.4
  14.0 48.7 %all-gather.8.cloned.1.call-done = f32[32,128,128]{2,1,0:T(8,128)} async-done(((f32[4,128,128]{2,1,0:T(8,128)}), f32[32,128,128]{2,1,0:T(8,128)}) %all-gather.8.cloned.1.call-update) | async-done | bytes 2097168 | tf_op jit(solution)/shard_map/all_gather | solution.py:13
  62.7 7.5 %while.28 = (s32[]{:T(128)}, f32[4,128,128]{2,1,0:T(8,128)S(1)}, s32[]{:T(128)}, f32[8,4,128,128]{3,2,1,0:T(8,128)}, s32[]{:T(128)}, /*index=5*/s32[]{:T(128)}) while((s32[]{:T(128)}, f32[4,128,128]{2,1,0:T(8,128)S(1)}, s32[]{:T(128)}, f32[8,4,128,128]{3,2,1,0:T(8,128)}, s32[]{:T(128)}, /*index=5*/s32[]{:T(128)}) %tuple.84), condition=%wide.region_1.2_spmd.clone, body=%wide.region_0.1_spmd.clone.sunk | while | flops 196612 | bytes 786533 | solution.py:23
  62.7 1.1 add_select_fusion.4
  63.8 1.0 add_select_fusion.4
  64.9 1.0 add_select_fusion.4
  66.0 1.0 add_select_fusion.4
  67.0 1.0 add_select_fusion.4
  68.1 1.0 add_select_fusion.4
  69.2 1.0 add_select_fusion.4
  70.5 42.1 %all-gather.6.cloned.1.call-done = bf16[2048,512]{1,0:T(8,128)(2,1)} async-done(((bf16[256,512]{1,0:T(8,128)(2,1)}), bf16[2048,512]{1,0:T(8,128)(2,1)}) %all-gather.6.cloned.1.call-update) | async-done | bytes 2097168 | tf_op jit(solution)/shard_map/all_gather | solution.py:68
  112.7 2.5 fusion.28
  115.5 0.8 copy.47
  116.4 2.7 convolution_bitcast_fusion
  119.2 0.8 copy-done.3
  120.2 1.2 convolution_bitcast_fusion.3
  121.4 0.8 fusion.3
  122.2 1.7 copy.52
  123.9 1.9 convolution_bitcast_fusion.1
  125.8 1.8 fusion.29
  127.6 2.5 convolution_convert_fusion
  130.2 34.2 %all-gather.10.cloned.1.call-done = f32[32,128,128]{2,1,0:T(8,128)} async-done(((f32[4,128,128]{2,1,0:T(8,128)}), f32[32,128,128]{2,1,0:T(8,128)}) %all-gather.10.cloned.1.call-update) | async-done | bytes 2097168 | tf_op jit(solution)/shard_map/all_gather | solution.py:13
  164.3 1.7 rev.3
  167.1 1.2 fusion.4
  168.2 0.8 copy.53
  170.0 84.8 %reduce-scatter.2.cloned.1.call-done = f32[256,512]{0,1:T(8,128)} async-done(((f32[2048,512]{0,1:T(8,128)}), f32[256,512]{0,1:T(8,128)}) %reduce-scatter.2.cloned.1.call-update) | async-done | bytes 524304 | tf_op jit(solution)/shard_map/reduce_scatter | solution.py:105
  254.8 2.0 copy.55
  256.8 19.4 %all-reduce.2.cloned.1.call-done = bf16[128,2048]{1,0:T(8,128)(2,1)} async-done(((bf16[128,2048]{1,0:T(8,128)(2,1)}), bf16[128,2048]{1,0:T(8,128)(2,1)}) %all-reduce.2.cloned.1.call-update) | async-done | bytes 524304 | tf_op jit(solution)/shard_map/psum | solution.py:72
  276.2 1.9 copy.120
  (54 shorter events, 5.0 us)
Async XLA Ops:
  7.2 105.5 %copy-start = (bf16[128,2048]{1,0:T(8,128)(2,1)S(1)}, bf16[128,2048]{1,0:T(8,128)(2,1)}, u32[]{:S(2)}) copy-start(bf16[128,2048]{1,0:T(8,128)(2,1)} %param.13) | copy-start | bytes 1572868
  7.2 55.6 %all-gather.8.cloned.1.call-start = ((), (), s32[]{:S(2)}) async-start(), calls=%async_computation.4 | async-start | bytes 2359296 | tf_op jit(solution)/shard_map/all_gather | solution.py:13
  8.3 2.6 copy-start.4
  10.2 102.5 %all-gather.6.cloned.1.call-start = ((), (), s32[]{:S(2)}) async-start(), calls=%async_computation.1 | async-start | bytes 2359296 | tf_op jit(solution)/shard_map/all_gather | solution.py:68
  10.9 153.4 %all-gather.10.cloned.1.call-start = ((), (), s32[]{:S(2)}) async-start(), calls=%async_computation.5 | async-start | bytes 2359296 | tf_op jit(solution)/shard_map/all_gather | solution.py:13
  12.2 0.6 copy-start.9
  14.0 56.2 %copy-start.2 = (f32[4,128,128]{2,1,0:T(8,128)S(1)}, f32[4,128,128]{2,1,0:T(8,128)}, u32[]{:S(2)}) copy-start(f32[4,128,128]{2,1,0:T(8,128)} %fusion.10) | copy-start | bytes 786436
  62.7 7.5 %copy-start.5 = (bf16[128,512]{1,0:T(8,128)(2,1)S(1)}, bf16[128,512]{1,0:T(8,128)(2,1)}, u32[]{:S(2)}) copy-start(bf16[128,512]{1,0:T(8,128)(2,1)} %param.9) | copy-start | bytes 393220
  115.3 3.7 %copy-start.6 = (bf16[1,128,4,128]{1,3,2,0:T(8,128)(2,1)}, bf16[1,128,4,128]{1,3,2,0:T(8,128)(2,1)S(1)}, u32[]{:S(2)}) copy-start(bf16[1,128,4,128]{1,3,2,0:T(8,128)(2,1)S(1)} %get-tuple-element.222) | copy-start | bytes 393220
  116.4 138.5 %reduce-scatter.2.cloned.1.call-start = ((), (), s32[]{:S(2)}) async-start(), calls=%async_computation.3 | async-start | bytes 4718592 | tf_op jit(solution)/shard_map/reduce_scatter | solution.py:105
  119.1 0.9 copy-start.3
  119.1 8.5 %copy-start.1 = (bf16[2048,512]{1,0:T(8,128)(2,1)S(1)}, bf16[2048,512]{1,0:T(8,128)(2,1)}, u32[]{:S(2)}) copy-start(bf16[2048,512]{1,0:T(8,128)(2,1)} %all-gather.6.cloned.1.call-done) | copy-start | bytes 6291460
  119.1 157.1 %all-reduce.2.cloned.1.call-start = ((), (), s32[]{:S(2)}) async-start(), calls=%async_computation.2 | async-start | bytes 1048576 | tf_op jit(solution)/shard_map/psum | solution.py:72
  120.2 2.0 copy-start.10
  166.1 2.9 %copy-start.7 = (f32[4,128,128]{2,1,0:T(8,128)S(1)}, f32[4,128,128]{2,1,0:T(8,128)}, u32[]{:S(2)}) copy-start(f32[4,128,128]{2,1,0:T(8,128)} %fusion.29) | copy-start | bytes 786436
  166.9 2.2 copy-start.8
Sparse Core Ops, SparseCore 0:
  10.7 51.9 all-gather.7
  64.9 47.7 all-gather.5
  116.5 47.8 all-gather.9
  167.8 86.9 reduce-scatter.1
  257.7 18.4 all-reduce.1
where the time goes:
time: 285 us
  waiting for transfers between devices  230 us (81%)
  matrix products  19.6 us (7%)
  between operations  14 us (5%)
  local copies, waits for them, and re-layouts  12.4 us (4%)
  other arithmetic  8.1 us (3%)
    reduce_scatter x1, waiting for transfers between devices, on_device(): lax.psum_scatter(lax.dot_general(grad_y, normed, (((0,), (0,)), ((), ()))...  84.8 us
    all_gather x2, waiting for transfers between devices, carried_in(): pieces = lax.all_gather(value, axis)  82.9 us
    all_gather x1, waiting for transfers between devices, on_device(): fore_weight = lax.all_gather(out_weight, 'seq', axis=0, tiled=True)  42.1 us
    psum x1, waiting for transfers between devices, on_device(): out_y = lax.psum(partial_out.astype(jnp.bfloat16), 'head')  19.4 us
    unnamed x27, local copies, waits for them, and re-layouts  8.63 us
    select_n x14, other arithmetic, turn(): return jnp.where(position < mine, longer, so_far)  7.89 us
  transfers between devices with their start and end apart: 5, of which 5 were waited for; matrix products, arithmetic and copies ran while one was open for 11% of the time, Pallas kernels for 0%

commit v1 on v0

--- a/solution.py
+++ b/solution.py
@@ -65,7 +65,12 @@
     contract_last = (((1,), (1,)), ((), ()))
     back_weight = lax.all_gather(out_weight, "seq", axis=0, tiled=True)
     grad_normed = jnp.dot(grad_y, back_weight, preferred_element_type=jnp.float32)
-    fore_weight = lax.all_gather(out_weight, "seq", axis=0, tiled=True)
+    ring = [out_weight]
+    for hop in range(7):
+        ring.append(lax.ppermute(ring[-1], "seq", [(dev, (dev + 1) % 8) for dev in range(8)]))
+    fore_weight = jnp.roll(
+        jnp.concatenate(ring[::-1], axis=0), (lax.axis_index("seq") + 1) * ring[0].shape[0], axis=0
+    )
     partial_out = lax.dot_general(
         normed, fore_weight, contract_last, preferred_element_type=jnp.float32
     )

time: 285 us -> 304 us (1.067)
  waiting for transfers between devices: 230 us -> 245 us
  local copies, waits for them, and re-layouts: 12.4 us -> 16.2 us
    ppermute x0 -> x7, waiting for transfers between devices: none -> 85.8 us  [on_device(): lax.ppermute(ring[-1], 'seq', [(dev, (dev + 1) % 8) for dev in range(8)])]
    reduce_scatter x1, waiting for transfers between devices: 84.8 us -> 47.8 us  [on_device(): lax.psum_scatter(lax.dot_general(grad_y, normed, (((0,), (0,)), ((), ()))...]
    all_gather x2, waiting for transfers between devices: 82.9 us -> 49.5 us  [carried_in(): pieces = lax.all_gather(value, axis)]
    unnamed x27 -> x34, local copies, waits for them, and re-layouts: 8.63 us -> 12.4 us
  transfers between devices with their start and end apart: 5 -> 12, of which waited for: 5 -> 11; matrix products, arithmetic and copies ran while one was open for 11% -> 10% of each run, Pallas kernels for 0% -> 0%
where the time goes in v1:
time: 304 us; the launch traced here: 303 us
  waiting for transfers between devices  245 us (81%)
  matrix products  17.7 us (6%)
  local copies, waits for them, and re-layouts  16.2 us (5%)
  between operations  14.1 us (5%)
  other arithmetic  8.07 us (3%)
    ppermute x7, waiting for transfers between devices, on_device(): lax.ppermute(ring[-1], 'seq', [(dev, (dev + 1) % 8) for dev in range(8)])  85.8 us
    all_gather x2, waiting for transfers between devices, carried_in(): pieces = lax.all_gather(value, axis)  49.5 us
    reduce_scatter x1, waiting for transfers between devices, on_device(): lax.psum_scatter(lax.dot_general(grad_y, normed, (((0,), (0,)), ((), ()))...  47.8 us
    all_gather x1, waiting for transfers between devices, on_device(): back_weight = lax.all_gather(out_weight, 'seq', axis=0, tiled=True)  42.2 us
    psum x1, waiting for transfers between devices, on_device(): out_y = lax.psum(partial_out.astype(jnp.bfloat16), 'head')  19.4 us
    unnamed x34, local copies, waits for them, and re-layouts  12.4 us
    select_n x14, other arithmetic, turn(): return jnp.where(position < mine, longer, so_far)  7.85 us
  transfers between devices with their start and end apart: 12, of which 11 were waited for; matrix products, arithmetic and copies ran while one was open for 10% of the time, Pallas kernels for 0%

profile of v1, /device:TPU:0, one launch (start us, length us, event | category | flops | bytes accessed | tf_op | source)
XLA Modules:
  0.0 303.4 jit_solution(9923882286460450453)
XLA Ops:
  7.2 1.1 copy.104
  8.3 1.8 fusion.11
  11.0 1.2 fusion.2
  12.2 1.1 convolution_bitcast_fusion.4
  13.3 49.4 %all-gather.8.cloned.1.call-done = f32[32,128,128]{2,1,0:T(8,128)} async-done(((f32[4,128,128]{2,1,0:T(8,128)}), f32[32,128,128]{2,1,0:T(8,128)}) %all-gather.8.cloned.1.call-update) | async-done | bytes 2097168 | tf_op jit(solution)/shard_map/all_gather | solution.py:13
  62.7 7.4 %while.28 = (s32[]{:T(128)}, f32[4,128,128]{2,1,0:T(8,128)S(1)}, s32[]{:T(128)}, f32[8,4,128,128]{3,2,1,0:T(8,128)}, s32[]{:T(128)}, /*index=5*/s32[]{:T(128)}) while((s32[]{:T(128)}, f32[4,128,128]{2,1,0:T(8,128)S(1)}, s32[]{:T(128)}, f32[8,4,128,128]{3,2,1,0:T(8,128)}, s32[]{:T(128)}, /*index=5*/s32[]{:T(128)}) %tuple.84), condition=%wide.region_1.2_spmd.clone, body=%wide.region_0.1_spmd.clone.sunk | while | flops 196612 | bytes 786525 | solution.py:23
  62.7 1.0 add_select_fusion.4
  63.8 1.0 add_select_fusion.4
  64.9 1.0 add_select_fusion.4
  65.9 1.0 add_select_fusion.4
  67.0 1.0 add_select_fusion.4
  68.1 1.0 add_select_fusion.4
  69.1 1.0 add_select_fusion.4
  70.5 42.2 %all-gather.6.cloned.1.call-done = bf16[2048,512]{1,0:T(8,128)(2,1)} async-done(((bf16[256,512]{1,0:T(8,128)(2,1)}), bf16[2048,512]{1,0:T(8,128)(2,1)}) %all-gather.6.cloned.1.call-update) | async-done | bytes 2097168 | tf_op jit(solution)/shard_map/all_gather | solution.py:66
  112.7 2.5 fusion.30
  116.4 2.6 convolution_bitcast_fusion
  119.8 9.6 %collective-permute-done = bf16[256,512]{1,0:T(8,128)(2,1)S(1)} collective-permute-done((bf16[256,512]{1,0:T(8,128)(2,1)S(1)}, bf16[256,512]{1,0:T(8,128)(2,1)S(1)}, u32[]{:S(2)}, u32[]{:S(2)}) %collective-permute-start) | collective-permute-done | bytes 262176 | tf_op jit(solution)/shard_map/ppermute | solution.py:70
  130.1 12.8 %collective-permute-done.1 = bf16[256,512]{1,0:T(8,128)(2,1)S(1)} collective-permute-done((bf16[256,512]{1,0:T(8,128)(2,1)S(1)}, bf16[256,512]{1,0:T(8,128)(2,1)S(1)}, u32[]{:S(2)}, u32[]{:S(2)}) %collective-permute-start.1) | collective-permute-done | bytes 262176 | tf_op jit(solution)/shard_map/ppermute | solution.py:70
  142.9 13.8 %collective-permute-done.2 = bf16[256,512]{1,0:T(8,128)(2,1)S(1)} collective-permute-done((bf16[256,512]{1,0:T(8,128)(2,1)S(1)}, bf16[256,512]{1,0:T(8,128)(2,1)S(1)}, u32[]{:S(2)}, u32[]{:S(2)}) %collective-permute-start.2) | collective-permute-done | bytes 262176 | tf_op jit(solution)/shard_map/ppermute | solution.py:70
  156.7 13.6 %collective-permute-done.3 = bf16[256,512]{1,0:T(8,128)(2,1)S(1)} collective-permute-done((bf16[256,512]{1,0:T(8,128)(2,1)S(1)}, bf16[256,512]{1,0:T(8,128)(2,1)S(1)}, u32[]{:S(2)}, u32[]{:S(2)}) %collective-permute-start.3) | collective-permute-done | bytes 262176 | tf_op jit(solution)/shard_map/ppermute | solution.py:70
  170.3 10.5 %collective-permute-done.4 = bf16[256,512]{1,0:T(8,128)(2,1)S(1)} collective-permute-done((bf16[256,512]{1,0:T(8,128)(2,1)S(1)}, bf16[256,512]{1,0:T(8,128)(2,1)S(1)}, u32[]{:S(2)}, u32[]{:S(2)}) %collective-permute-start.4) | collective-permute-done | bytes 262176 | tf_op jit(solution)/shard_map/ppermute | solution.py:70
  180.8 9.3 %collective-permute-done.5 = bf16[256,512]{1,0:T(8,128)(2,1)} collective-permute-done((bf16[256,512]{1,0:T(8,128)(2,1)S(1)}, bf16[256,512]{1,0:T(8,128)(2,1)}, u32[]{:S(2)}, u32[]{:S(2)}) %collective-permute-start.5) | collective-permute-done | bytes 262176 | tf_op jit(solution)/shard_map/ppermute | solution.py:70
  190.1 16.2 %collective-permute-done.6 = bf16[256,512]{1,0:T(8,128)(2,1)} collective-permute-done((bf16[256,512]{1,0:T(8,128)(2,1)}, bf16[256,512]{1,0:T(8,128)(2,1)}, u32[]{:S(2)}, u32[]{:S(2)}) %collective-permute-start.6) | collective-permute-done | bytes 262176 | tf_op jit(solution)/shard_map/ppermute | solution.py:70
  210.6 2.0 copy-done.3
  215.8 3.2 %convolution_convert_fusion = bf16[128,2048]{1,0:T(8,128)(2,1)} fusion(bf16[128,512]{0,1:T(8,128)(2,1)S(1)} %bitcast.125, bf16[4096,512]{1,0:T(8,128)(2,1)} %copy-done.3, s32[]{:T(128)S(6)} %select_n.64), kind=kOutput, calls=%fused_computation.3 | convolution fusion | flops 268697600 | bytes 2752516 | tf_op jit(solution)/shard_map/dot_general | solution.py:74
  219.1 1.8 rev.3
  221.9 1.2 fusion.5
  223.8 1.2 fusion.6
  225.8 47.8 %reduce-scatter.2.cloned.1.call-done = f32[256,512]{0,1:T(8,128)} async-done(((f32[2048,512]{0,1:T(8,128)}), f32[256,512]{0,1:T(8,128)}) %reduce-scatter.2.cloned.1.call-update) | async-done | bytes 524304 | tf_op jit(solution)/shard_map/reduce_scatter | solution.py:110
  273.6 2.0 copy.55
  275.6 19.4 %all-reduce.2.cloned.1.call-done = bf16[128,2048]{1,0:T(8,128)(2,1)} async-done(((bf16[128,2048]{1,0:T(8,128)(2,1)}), bf16[128,2048]{1,0:T(8,128)(2,1)}) %all-reduce.2.cloned.1.call-update) | async-done | bytes 524304 | tf_op jit(solution)/shard_map/psum | solution.py:77
  295.0 1.9 copy.135
  (76 shorter events, 14.3 us)
Async XLA Ops:
  7.2 105.5 %copy-start = (bf16[128,2048]{1,0:T(8,128)(2,1)S(1)}, bf16[128,2048]{1,0:T(8,128)(2,1)}, u32[]{:S(2)}) copy-start(bf16[128,2048]{1,0:T(8,128)(2,1)} %param.13) | copy-start | bytes 1572868
  7.2 63.1 %copy-start.5 = (bf16[128,512]{1,0:T(8,128)(2,1)S(1)}, bf16[128,512]{1,0:T(8,128)(2,1)}, u32[]{:S(2)}) copy-start(bf16[128,512]{1,0:T(8,128)(2,1)} %param.9) | copy-start | bytes 393220
  7.2 55.6 %all-gather.8.cloned.1.call-start = ((), (), s32[]{:S(2)}) async-start(), calls=%async_computation.4 | async-start | bytes 2359296 | tf_op jit(solution)/shard_map/all_gather | solution.py:13
  10.1 60.1 %copy-start.2 = (f32[4,128,128]{2,1,0:T(8,128)S(1)}, f32[4,128,128]{2,1,0:T(8,128)}, u32[]{:S(2)}) copy-start(f32[4,128,128]{2,1,0:T(8,128)} %fusion.11) | copy-start | bytes 786436
  10.1 102.5 %all-gather.6.cloned.1.call-start = ((), (), s32[]{:S(2)}) async-start(), calls=%async_computation.2 | async-start | bytes 2359296 | tf_op jit(solution)/shard_map/all_gather | solution.py:66
  10.9 208.2 %all-gather.10.cloned.1.call-start = ((), (), s32[]{:S(2)}) async-start(), calls=%async_computation.5 | async-start | bytes 2359296 | tf_op jit(solution)/shard_map/all_gather | solution.py:13
  116.4 157.2 %reduce-scatter.2.cloned.1.call-start = ((), (), s32[]{:S(2)}) async-start(), calls=%async_computation.3 | async-start | bytes 4718592 | tf_op jit(solution)/shard_map/reduce_scatter | solution.py:110
  116.4 2.7 copy-start.1
  119.1 175.9 %all-reduce.2.cloned.1.call-start = ((), (), s32[]{:S(2)}) async-start(), calls=%async_computation.1 | async-start | bytes 1048576 | tf_op jit(solution)/shard_map/psum | solution.py:77
  119.2 10.2 %collective-permute-start = (bf16[256,512]{1,0:T(8,128)(2,1)S(1)}, bf16[256,512]{1,0:T(8,128)(2,1)S(1)}, u32[]{:S(2)}, u32[]{:S(2)}) collective-permute-start(bf16[256,512]{1,0:T(8,128)(2,1)S(1)} %copy-done.1), channel_id=1, source_target_pairs={{0,2},{2,4},{4,6},{6,8},{8,10},{10,12},{12,14},{14,0},{1,3},{3,5},... | collective-permute-start | bytes 786440 | tf_op jit(solution)/shard_map/ppermute | solution.py:70
  129.3 13.6 %collective-permute-start.1 = (bf16[256,512]{1,0:T(8,128)(2,1)S(1)}, bf16[256,512]{1,0:T(8,128)(2,1)S(1)}, u32[]{:S(2)}, u32[]{:S(2)}) collective-permute-start(bf16[256,512]{1,0:T(8,128)(2,1)S(1)} %collective-permute-done), channel_id=1, source_target_pairs={{0,2},{2,4},{4,6},{6,8},{8,10},{10,12},{12,14},{14,0},{1,3},{3,5},... | collective-permute-start | bytes 786440 | tf_op jit(solution)/shard_map/ppermute | solution.py:70
  142.9 13.8 %collective-permute-start.2 = (bf16[256,512]{1,0:T(8,128)(2,1)S(1)}, bf16[256,512]{1,0:T(8,128)(2,1)S(1)}, u32[]{:S(2)}, u32[]{:S(2)}) collective-permute-start(bf16[256,512]{1,0:T(8,128)(2,1)S(1)} %collective-permute-done.1), channel_id=1, source_target_pairs={{0,2},{2,4},{4,6},{6,8},{8,10},{10,12},{12,14},{14,0},{1,3},{3,5},... | collective-permute-start | bytes 786440 | tf_op jit(solution)/shard_map/ppermute | solution.py:70
  156.7 13.6 %collective-permute-start.3 = (bf16[256,512]{1,0:T(8,128)(2,1)S(1)}, bf16[256,512]{1,0:T(8,128)(2,1)S(1)}, u32[]{:S(2)}, u32[]{:S(2)}) collective-permute-start(bf16[256,512]{1,0:T(8,128)(2,1)S(1)} %collective-permute-done.2), channel_id=1, source_target_pairs={{0,2},{2,4},{4,6},{6,8},{8,10},{10,12},{12,14},{14,0},{1,3},{3,5},... | collective-permute-start | bytes 786440 | tf_op jit(solution)/shard_map/ppermute | solution.py:70
  170.3 10.5 %collective-permute-start.4 = (bf16[256,512]{1,0:T(8,128)(2,1)S(1)}, bf16[256,512]{1,0:T(8,128)(2,1)S(1)}, u32[]{:S(2)}, u32[]{:S(2)}) collective-permute-start(bf16[256,512]{1,0:T(8,128)(2,1)S(1)} %collective-permute-done.3), channel_id=1, source_target_pairs={{0,2},{2,4},{4,6},{6,8},{8,10},{10,12},{12,14},{14,0},{1,3},{3,5},... | collective-permute-start | bytes 786440 | tf_op jit(solution)/shard_map/ppermute | solution.py:70
  180.8 9.3 %collective-permute-start.5 = (bf16[256,512]{1,0:T(8,128)(2,1)S(1)}, bf16[256,512]{1,0:T(8,128)(2,1)}, u32[]{:S(2)}, u32[]{:S(2)}) collective-permute-start(bf16[256,512]{1,0:T(8,128)(2,1)S(1)} %collective-permute-done.4), channel_id=1, source_target_pairs={{0,2},{2,4},{4,6},{6,8},{8,10},{10,12},{12,14},{14,0},{1,3},{3,5},... | collective-permute-start | bytes 786440 | tf_op jit(solution)/shard_map/ppermute | solution.py:70
  190.1 16.3 %collective-permute-start.6 = (bf16[256,512]{1,0:T(8,128)(2,1)}, bf16[256,512]{1,0:T(8,128)(2,1)}, u32[]{:S(2)}, u32[]{:S(2)}) collective-permute-start(bf16[256,512]{1,0:T(8,128)(2,1)} %collective-permute-done.5), channel_id=1, source_target_pairs={{0,2},{2,4},{4,6},{6,8},{8,10},{10,12},{12,14},{14,0},{1,3},{3,5},... | collective-permute-start | bytes 786440 | tf_op jit(solution)/shard_map/ppermute | solution.py:70
  190.1 22.5 %copy-start.4 = (bf16[128,512]{1,0:T(8,128)(2,1)S(1)}, bf16[128,512]{1,0:T(8,128)(2,1)}, u32[]{:S(2)}) copy-start(bf16[128,512]{1,0:T(8,128)(2,1)} %param.11) | copy-start | bytes 393220
  210.6 2.0 copy-start.3
  219.1 4.7 %copy-start.6 = (bf16[128,512]{1,0:T(8,128)(2,1)S(1)}, bf16[128,512]{1,0:T(8,128)(2,1)}, u32[]{:S(2)}) copy-start(bf16[128,512]{1,0:T(8,128)(2,1)} %param.10) | copy-start | bytes 393220
Sparse Core Ops, SparseCore 0:
  10.7 51.9 all-gather.7
  64.9 47.7 all-gather.5
  116.5 58.8 all-gather.9
  178.9 94.6 reduce-scatter.1
  276.5 18.4 all-reduce.1
